TPU v7x, 256 devices: a whole 4x4x8 slice. The times are simulated.
256 devices in a mesh: loop: 16 (over z, x_lo), row: 4 (over x_hi, core), col: 4 (over y).
Axes of the slice: x: 4 (x_hi: 2, x_lo: 2; x = x_hi * 2 + x_lo), y: 4, z: 8, core: 2. Of those that a mesh axis runs over, the one named last changes fastest.
Arguments:
- interval_blocks: bfloat16 [16, 4, 2048, 2048], P('loop', None, 'row', 'col'), may hold values from -0.15625 to 0.15625
- interval_pivots: int32 [16, 3, 2048], P('loop'), may hold values from 0 to 2047, each once within a row
- boundary_pivots: int32 [16, 2048], replicated, may hold values from 0 to 2047, each once within a row
- interval_residuals: bfloat16 [16, 4, 2048], P('loop', None, ('row', 'col')), may hold values from -0.23925781 to 0.23925781
Outputs:
- reduced_block: bfloat16 [16, 2048, 2048], P('loop', 'row', 'col')
- reduced_rhs: float32 [16, 2048], P('loop', ('row', 'col'))
Inputs may be any that keep to these rules, and one draw needn't show every extreme that they name: Each row of interval_pivots is a permutation of 0 to 2047. Each row of boundary_pivots is a permutation of 0 to 2047.
All inputs are finite; a program needn't handle non-finite values.
Results may differ from a plain program's by a relative error of at most 0.018.
Values may be sent and summed in bfloat16 or wider, within the bound.
A program may use at most 64 MiB of HBM per device.

v0:
```python
import jax
import jax.numpy as jnp
from jax import lax
from jax.sharding import PartitionSpec as P


def from_behind(value, axis, by):
    devices = lax.axis_size(axis)
    return lax.ppermute(value, axis, [(i, (i + by) % devices) for i in range(devices)])


def compose(left_block, right_block, right_vector, pivots, added):
    column_panel = lax.all_gather(right_block, "row", axis=0, tiled=True)
    full_vector = lax.all_gather(right_vector, ("row", "col"), axis=0, tiled=True)
    permuted = jnp.take(column_panel, pivots, axis=0)
    moved = jnp.take(full_vector, pivots, axis=0)
    segment = lax.all_gather(left_block, "col", axis=1, tiled=True)
    product = jnp.dot(segment, permuted, preferred_element_type=jnp.float32)
    applied = jnp.dot(segment, moved, preferred_element_type=jnp.float32)
    share_size = added.shape[0]
    own_part = lax.dynamic_slice_in_dim(applied, lax.axis_index("col") * share_size, share_size, 0)
    return (product, own_part + added.astype(jnp.float32))


def shards(interval_blocks, interval_pivots, boundary_pivots, interval_residuals):
    blocks = interval_blocks[0]
    pivot_rows = interval_pivots[0]
    residuals = interval_residuals[0]
    matrix = blocks[0]
    vector = residuals[0]
    for interval in range(1, blocks.shape[0]):
        product, applied = compose(
            blocks[interval], matrix, vector, pivot_rows[interval - 1], residuals[interval]
        )
        matrix = product.astype(jnp.bfloat16)
        vector = applied.astype(jnp.bfloat16)
    position = lax.axis_index("loop")
    count_loop = lax.axis_size("loop")
    own_pivots = lax.dynamic_index_in_dim(boundary_pivots, position, 0, keepdims=False)
    back_pivots = lax.dynamic_index_in_dim(
        boundary_pivots, (position + count_loop - 1) % count_loop, 0, keepdims=False
    )
    earlier, earlier_vector = from_behind((matrix, vector), "loop", 1)
    product, applied = compose(matrix, earlier, earlier_vector, own_pivots, vector)
    halved = product.astype(jnp.bfloat16)
    halved_vector = applied.astype(jnp.bfloat16)
    distant, distant_vector = from_behind((halved, halved_vector), "loop", 2)
    reduced, reduced_vector = compose(halved, distant, distant_vector, back_pivots, halved_vector)
    return (reduced.astype(jnp.bfloat16)[None], reduced_vector[None])


def solution(mesh):
    placed = (
        P("loop", None, "row", "col"),
        P("loop", None, None),
        P(),
        P("loop", None, ("row", "col")),
    )
    return jax.shard_map(
        shards,
        mesh=mesh,
        in_specs=placed,
        out_specs=(P("loop", "row", "col"), P("loop", ("row", "col"))),
        check_vma=False,
    )
```

profile of v0, /device:TPU:8, one launch (start us, length us, event | category | flops | bytes accessed | tf_op | source)
XLA Modules:
  0.0 394.3 jit_solution(15672747446238209155)
XLA Ops:
  7.2 2.9 fusion.83
  10.9 34.3 %all-gather.4 = bf16[1,1,2048]{2,1,0:T(2,128)(2,1)S(1)} all-gather(bf16[1,1,128]{2,1,0:T(2,128)(2,1)S(1)} %slice.51), channel_id=6, replica_groups=mesh['loop'=16,'row'=4,'col'=4] {'row','col'}, dimensions={2}, use_global_device_ids=true | all-gather | bytes 4352 | tf_op jit(solution)/shard_map/all_gather | solution.py:14
  45.3 13.1 %gather_fusion.5 = bf16[2048]{0:T(1024)(128)(2,1)S(1)} fusion(bf16[2048]{0:T(1024)(128)(2,1)S(1)} %reduce, s32[2048]{0:T(1024)S(1)} %fusion.68), kind=kCustom, calls=%fused_computation.1.clone | custom fusion | bytes 16384 | tf_op jit(solution)/shard_map/jit(_take)/gather | solution.py:16
  58.5 9.5 %gather_fusion = bf16[2048,512]{1,0:T(8,128)(2,1)S(1)} fusion(bf16[2048,512]{1,0:T(8,128)(2,1)} %bitcast.80, s32[2048]{0:T(1024)S(1)} %fusion.68), kind=kCustom, calls=%fused_computation.clone | custom fusion | bytes 4202496 | tf_op jit(solution)/shard_map/jit(_take)/gather | solution.py:15
  67.9 8.3 %all-gather.34.cloned.1.call-done = bf16[1,1,512,2048]{3,2,1,0:T(8,128)(2,1)} async-done(((bf16[1,1,512,512]{3,2,1,0:T(8,128)(2,1)}), bf16[1,1,512,2048]{3,2,1,0:T(8,128)(2,1)}) %all-gather.34.cloned.1.call-update) | async-done | bytes 2097168 | tf_op jit(solution)/shard_map/all_gather | solution.py:17
  76.3 4.1 %fusion.55 = bf16[512,512]{0,1:T(8,128)(2,1)} fusion(bf16[1,1,512,2048]{3,2,1,0:T(8,128)(2,1)} %all-gather.34.cloned.1.call-done, bf16[2048,512]{1,0:T(8,128)(2,1)S(1)} %gather_fusion, pred[2048]{0:T(1024)(128)(4,1)S(1)} %get-tuple-element.13), kind=kOutput, calls=%fused_computation.41 | convolution fusion | flops 1075052544 | bytes 4720640 | tf_op jit(solution)/shard_map/dot_general | solution.py:18
  81.0 2.2 fusion.8
  83.3 33.7 %all-gather.5 = bf16[16,1,128]{2,1,0:T(2,128)(2,1)S(1)} all-gather(bf16[1,1,128]{2,1,0:T(2,128)(2,1)S(1)} %fusion.77), channel_id=1, replica_groups=mesh['loop'=16,'row'=4,'col'=4] {'row','col'}, dimensions={0}, use_global_device_ids=true | all-gather | bytes 4352 | tf_op jit(solution)/shard_map/all_gather | solution.py:14
  117.0 13.1 %gather_fusion.6 = bf16[2048]{0:T(1024)(128)(2,1)S(1)} fusion(bf16[2048]{0:T(1024)(128)(2,1)S(1)} %bitcast.77, s32[2048]{0:T(1024)S(1)} %fusion.69), kind=kCustom, calls=%fused_computation.6.clone | custom fusion | bytes 16384 | tf_op jit(solution)/shard_map/jit(_take)/gather | solution.py:16
  130.1 2.9 copy.8
  133.0 9.2 %gather_fusion.1 = bf16[2048,512]{1,0:T(8,128)(2,1)} fusion(bf16[2048,512]{1,0:T(8,128)(2,1)S(1)} %copy.8, s32[2048]{0:T(1024)S(1)} %fusion.69), kind=kCustom, calls=%fused_computation.2.clone | custom fusion | bytes 4202496 | tf_op jit(solution)/shard_map/jit(_take)/gather | solution.py:15
  144.3 4.8 %fusion.50 = bf16[512,512]{0,1:T(8,128)(2,1)} fusion(bf16[1,1,512,2048]{3,2,1,0:T(8,128)(2,1)} %all-gather.36.cloned.1.call-done, bf16[2048,512]{1,0:T(8,128)(2,1)} %gather_fusion.1, pred[2048]{0:T(1024)(128)(4,1)S(1)} %get-tuple-element.11), kind=kOutput, calls=%fused_computation.40 | convolution fusion | flops 1075052544 | bytes 4720640 | tf_op jit(solution)/shard_map/dot_general | solution.py:18
  150.5 33.7 %all-gather.6 = bf16[16,1,128]{2,1,0:T(2,128)(2,1)S(1)} all-gather(bf16[1,1,128]{2,1,0:T(2,128)(2,1)S(1)} %fusion.75), channel_id=1, replica_groups=mesh['loop'=16,'row'=4,'col'=4] {'row','col'}, dimensions={0}, use_global_device_ids=true | all-gather | bytes 4352 | tf_op jit(solution)/shard_map/all_gather | solution.py:14
  184.2 13.1 %gather_fusion.7 = bf16[2048]{0:T(1024)(128)(2,1)S(1)} fusion(bf16[2048]{0:T(1024)(128)(2,1)S(1)} %bitcast.78, s32[2048]{0:T(1024)S(1)} %fusion.70), kind=kCustom, calls=%fused_computation.7.clone | custom fusion | bytes 16384 | tf_op jit(solution)/shard_map/jit(_take)/gather | solution.py:16
  197.4 2.9 copy.9
  200.2 9.2 %gather_fusion.2 = bf16[2048,512]{1,0:T(8,128)(2,1)} fusion(bf16[2048,512]{1,0:T(8,128)(2,1)S(1)} %copy.9, s32[2048]{0:T(1024)S(1)} %fusion.70), kind=kCustom, calls=%fused_computation.3.clone | custom fusion | bytes 4202496 | tf_op jit(solution)/shard_map/jit(_take)/gather | solution.py:15
  209.4 3.7 all-gather.38.cloned.1.call-done
  213.1 4.0 %fusion.45 = bf16[512,512]{0,1:T(8,128)(2,1)S(1)} fusion(bf16[1,1,512,2048]{3,2,1,0:T(8,128)(2,1)} %all-gather.38.cloned.1.call-done, bf16[2048,512]{1,0:T(8,128)(2,1)} %gather_fusion.2, pred[2048]{0:T(1024)(128)(4,1)S(1)} %get-tuple-element.9), kind=kOutput, calls=%fused_computation.39 | convolution fusion | flops 1075052544 | bytes 4720640 | tf_op jit(solution)/shard_map/dot_general | solution.py:18
  218.7 14.7 %collective-permute-done = bf16[512,512]{0,1:T(8,128)(2,1)S(1)} collective-permute-done((bf16[512,512]{0,1:T(8,128)(2,1)S(1)}, bf16[512,512]{0,1:T(8,128)(2,1)S(1)}, u32[]{:S(2)}, u32[]{:S(2)}) %collective-permute-start) | collective-permute-done | bytes 524320 | tf_op jit(solution)/shard_map/ppermute | solution.py:9
  236.9 5.6 %collective-permute-done.2 = bf16[128]{0:T(256)(128)(2,1)S(1)} collective-permute-done((bf16[128]{0:T(256)(128)(2,1)S(1)}, bf16[128]{0:T(256)(128)(2,1)S(1)}, u32[]{:S(2)}, u32[]{:S(2)}) %collective-permute-start.2) | collective-permute-done | bytes 288 | tf_op jit(solution)/shard_map/ppermute | solution.py:9
  242.5 33.6 %all-gather.7 = bf16[16,1,128]{2,1,0:T(2,128)(2,1)S(1)} all-gather(bf16[1,1,128]{2,1,0:T(2,128)(2,1)S(1)} %bitcast.97), channel_id=1, replica_groups=mesh['loop'=16,'row'=4,'col'=4] {'row','col'}, dimensions={0}, use_global_device_ids=true | all-gather | bytes 4352 | tf_op jit(solution)/shard_map/all_gather | solution.py:14
  276.2 13.1 %gather_fusion.8 = bf16[2048]{0:T(1024)(128)(2,1)S(1)} fusion(bf16[2048]{0:T(1024)(128)(2,1)S(1)} %bitcast.79, s32[2048]{0:T(1024)S(1)} %fusion.71), kind=kCustom, calls=%fused_computation.8.clone | custom fusion | bytes 16384 | tf_op jit(solution)/shard_map/jit(_take)/gather | solution.py:16
  289.3 2.9 copy.10
  292.2 9.2 %gather_fusion.3 = bf16[2048,512]{1,0:T(8,128)(2,1)} fusion(bf16[2048,512]{1,0:T(8,128)(2,1)S(1)} %copy.10, s32[2048]{0:T(1024)S(1)} %fusion.71), kind=kCustom, calls=%fused_computation.4.clone | custom fusion | bytes 4202496 | tf_op jit(solution)/shard_map/jit(_take)/gather | solution.py:15
  301.4 4.5 %fusion.24 = bf16[512,512]{1,0:T(8,128)(2,1)} fusion(bf16[512,2048]{0,1:T(8,128)(2,1)} %all-gather.24.cloned.1.call-done, bf16[2048,512]{1,0:T(8,128)(2,1)} %gather_fusion.3, pred[2048]{0:T(1024)(128)(4,1)S(1)} %get-tuple-element.7), kind=kOutput, calls=%fused_computation.34 | convolution fusion | flops 1075052544 | bytes 4720640 | tf_op jit(solution)/shard_map/dot_general | solution.py:18
  306.1 12.5 %collective-permute-done.1 = bf16[512,512]{1,0:T(8,128)(2,1)S(1)} collective-permute-done((bf16[512,512]{1,0:T(8,128)(2,1)}, bf16[512,512]{1,0:T(8,128)(2,1)S(1)}, u32[]{:S(2)}, u32[]{:S(2)}) %collective-permute-start.1) | collective-permute-done | bytes 524320 | tf_op jit(solution)/shard_map/ppermute | solution.py:9
  319.9 4.7 %collective-permute-done.3 = bf16[128]{0:T(256)(128)(2,1)S(1)} collective-permute-done((bf16[128]{0:T(256)(128)(2,1)S(1)}, bf16[128]{0:T(256)(128)(2,1)S(1)}, u32[]{:S(2)}, u32[]{:S(2)}) %collective-permute-start.3) | collective-permute-done | bytes 288 | tf_op jit(solution)/shard_map/ppermute | solution.py:9
  324.7 33.6 %all-gather.8 = bf16[16,1,128]{2,1,0:T(2,128)(2,1)S(1)} all-gather(bf16[1,1,128]{2,1,0:T(2,128)(2,1)S(1)} %bitcast.96), channel_id=1, replica_groups=mesh['loop'=16,'row'=4,'col'=4] {'row','col'}, dimensions={0}, use_global_device_ids=true | all-gather | bytes 4352 | tf_op jit(solution)/shard_map/all_gather | solution.py:14
  358.3 13.1 %gather_fusion.9 = bf16[2048]{0:T(1024)(128)(2,1)S(1)} fusion(bf16[2048]{0:T(1024)(128)(2,1)S(1)} %bitcast.76, s32[2048]{0:T(1024)S(1)} %fusion.72), kind=kCustom, calls=%fused_computation.9.clone | custom fusion | bytes 16384 | tf_op jit(solution)/shard_map/jit(_take)/gather | solution.py:16
  371.5 2.2 fusion.86
  374.3 9.4 %gather_fusion.4 = bf16[2048,512]{1,0:T(8,128)(2,1)S(1)} fusion(bf16[2048,512]{1,0:T(8,128)(2,1)} %all-gather.30.cloned.1.call-done, s32[2048]{0:T(1024)S(1)} %fusion.72), kind=kCustom, calls=%fused_computation.5.clone | custom fusion | bytes 4202496 | tf_op jit(solution)/shard_map/jit(_take)/gather | solution.py:15
  383.8 3.7 fusion.60
  (79 shorter events, 12.4 us)
Async XLA Ops:
  7.2 3.7 copy-start.7
  7.2 38.1 %copy-start.6 = (s32[1,3,2048]{2,0,1:T(1,128)S(1)}, s32[1,3,2048]{2,0,1:T(1,128)}, u32[]{:S(2)}) copy-start(s32[1,3,2048]{2,0,1:T(1,128)} %param.9) | copy-start | bytes 73732
  7.2 51.3 %all-gather.32.cloned.1.call-start = ((), (), s32[]{:S(2)}) async-start(), calls=%async_computation.6 | async-start | bytes 2621440 | tf_op jit(solution)/shard_map/all_gather | solution.py:13
  10.1 66.1 %all-gather.34.cloned.1.call-start = ((), (), s32[]{:S(2)}) async-start(), calls=%async_computation.7 | async-start | bytes 2621440 | tf_op jit(solution)/shard_map/all_gather | solution.py:17
  10.9 119.3 %all-gather.20.cloned.1.call-start = ((), (), s32[]{:S(2)}) async-start(), calls=%async_computation | async-start | bytes 2621440 | tf_op jit(solution)/shard_map/all_gather | solution.py:13
  80.3 63.9 %all-gather.36.cloned.1.call-start = ((), (), s32[]{:S(2)}) async-start(), calls=%async_computation.8 | async-start | bytes 2621440 | tf_op jit(solution)/shard_map/all_gather | solution.py:17
  80.9 116.4 %all-gather.22.cloned.1.call-start = ((), (), s32[]{:S(2)}) async-start(), calls=%async_computation.1 | async-start | bytes 2621440 | tf_op jit(solution)/shard_map/all_gather | solution.py:13
  144.3 5.5 %copy-start.2 = (bf16[1,1,512,2048]{3,2,1,0:T(8,128)(2,1)S(1)}, bf16[1,1,512,2048]{3,2,1,0:T(8,128)(2,1)}, u32[]{:S(2)}) copy-start(bf16[1,1,512,2048]{3,2,1,0:T(8,128)(2,1)} %all-gather.36.cloned.1.call-done) | copy-start | bytes 6291460
  149.1 63.9 %all-gather.38.cloned.1.call-start = ((), (), s32[]{:S(2)}) async-start(), calls=%async_computation.9 | async-start | bytes 2621440 | tf_op jit(solution)/shard_map/all_gather | solution.py:17
  149.7 139.6 %all-gather.26.cloned.1.call-start = ((), (), s32[]{:S(2)}) async-start(), calls=%async_computation.3 | async-start | bytes 2621440 | tf_op jit(solution)/shard_map/all_gather | solution.py:13
  213.1 22.8 %copy-start.1 = (bf16[1,1,512,2048]{3,2,1,0:T(8,128)(2,1)S(1)}, bf16[1,1,512,2048]{3,2,1,0:T(8,128)(2,1)}, u32[]{:S(2)}) copy-start(bf16[1,1,512,2048]{3,2,1,0:T(8,128)(2,1)} %all-gather.38.cloned.1.call-done) | copy-start | bytes 6291460
  217.1 17.1 %copy-start.3 = (bf16[512,512]{0,1:T(8,128)(2,1)}, bf16[512,512]{0,1:T(8,128)(2,1)S(1)}, u32[]{:S(2)}) copy-start(bf16[512,512]{0,1:T(8,128)(2,1)S(1)} %fusion.45) | copy-start | bytes 1572868
  217.1 16.2 %collective-permute-start = (bf16[512,512]{0,1:T(8,128)(2,1)S(1)}, bf16[512,512]{0,1:T(8,128)(2,1)S(1)}, u32[]{:S(2)}, u32[]{:S(2)}) collective-permute-start(bf16[512,512]{0,1:T(8,128)(2,1)S(1)} %fusion.45), channel_id=1, source_target_pairs={{0,16},{16,32},{32,48},{48,64},{64,80},{80,96},{96,112},{112,128},... | collective-permute-start | bytes 1572872 | tf_op jit(solution)/shard_map/ppermute | solution.py:9
  233.4 0.8 copy-start.4
  234.2 67.2 %all-gather.24.cloned.1.call-start = ((), (), s32[]{:S(2)}) async-start(), calls=%async_computation.2 | async-start | bytes 2621440 | tf_op jit(solution)/shard_map/all_gather | solution.py:17
  235.0 136.5 %all-gather.28.cloned.1.call-start = ((), (), s32[]{:S(2)}) async-start(), calls=%async_computation.4 | async-start | bytes 2621440 | tf_op jit(solution)/shard_map/all_gather | solution.py:17
  236.7 5.8 %collective-permute-start.2 = (bf16[128]{0:T(256)(128)(2,1)S(1)}, bf16[128]{0:T(256)(128)(2,1)S(1)}, u32[]{:S(2)}, u32[]{:S(2)}) collective-permute-start(bf16[128]{0:T(256)(128)(2,1)S(1)} %fusion.73), channel_id=1, source_target_pairs={{0,16},{16,32},{32,48},{48,64},{64,80},{80,96},{96,112},{112,128},... | collective-permute-start | bytes 776 | tf_op jit(solution)/shard_map/ppermute | solution.py:9
  301.4 18.0 %copy-start = (bf16[512,2048]{0,1:T(8,128)(2,1)S(1)}, bf16[512,2048]{0,1:T(8,128)(2,1)}, u32[]{:S(2)}) copy-start(bf16[512,2048]{0,1:T(8,128)(2,1)} %all-gather.24.cloned.1.call-done) | copy-start | bytes 6291460
  305.9 68.4 %all-gather.30.cloned.1.call-start = ((), (), s32[]{:S(2)}) async-start(), calls=%async_computation.5 | async-start | bytes 2621440 | tf_op jit(solution)/shard_map/all_gather | solution.py:13
  306.0 12.6 %collective-permute-start.1 = (bf16[512,512]{1,0:T(8,128)(2,1)}, bf16[512,512]{1,0:T(8,128)(2,1)S(1)}, u32[]{:S(2)}, u32[]{:S(2)}) collective-permute-start(bf16[512,512]{1,0:T(8,128)(2,1)} %fusion.24), channel_id=1, source_target_pairs={{0,32},{16,48},{32,64},{48,80},{64,96},{80,112},{96,128},{112,144}... | collective-permute-start | bytes 1572872 | tf_op jit(solution)/shard_map/ppermute | solution.py:9
  318.6 0.8 copy-start.5
  319.9 4.8 %collective-permute-start.3 = (bf16[128]{0:T(256)(128)(2,1)S(1)}, bf16[128]{0:T(256)(128)(2,1)S(1)}, u32[]{:S(2)}, u32[]{:S(2)}) collective-permute-start(bf16[128]{0:T(256)(128)(2,1)S(1)} %add_convert_fusion), channel_id=1, source_target_pairs={{0,32},{16,48},{32,64},{48,80},{64,96},{80,112},{96,128},{112,144}... | collective-permute-start | bytes 776 | tf_op jit(solution)/shard_map/ppermute | solution.py:9
Sparse Core Ops, SparseCore 0:
  10.4 32.0 all-gather.31
  44.3 31.9 all-gather.33
  80.5 30.1 all-gather.19
  112.3 31.9 all-gather.35
  149.3 30.1 all-gather.21
  181.1 31.9 all-gather.37
  234.3 29.7 all-gather.25
  266.5 31.9 all-gather.23
  306.0 31.8 all-gather.27
  339.6 30.1 all-gather.29
where the time goes:
time: 395 us; the launch traced here: 394 us
  blocking collectives  169 us (43%)
  local copies, waits for them, and re-layouts  126 us (32%)
  waiting for transfers between devices  54.3 us (14%)
  matrix products  27.2 us (7%)
  between operations  14.6 us (4%)
    all_gather x5, blocking collectives, compose(): lax.all_gather(right_vector, ('row', 'col'), axis=0, tiled=True)  169 us
    gather x5, local copies, waits for them, and re-layouts, compose(): moved = jnp.take(full_vector, pivots, axis=0)  65.4 us
    gather x5, local copies, waits for them, and re-layouts, compose(): permuted = jnp.take(column_panel, pivots, axis=0)  46.4 us
    ppermute x4, waiting for transfers between devices, from_behind(): lax.ppermute(value, axis, [(i, (i + by) % devices) for i in range(devices)])  37.5 us
    dot_general x5, matrix products, compose(): product = jnp.dot(segment, permuted, preferred_element_type=jnp.float32)  21.1 us
    all_gather x5, waiting for transfers between devices, compose(): segment = lax.all_gather(left_block, 'col', axis=1, tiled=True)  14.1 us
    all_gather x3, local copies, waits for them, and re-layouts, compose(): column_panel = lax.all_gather(right_block, 'row', axis=0, tiled=True)  8.65 us
  transfers between devices with their start and end apart: 14, of which 7 were waited for; matrix products, arithmetic and copies ran while one was open for 30% of the time, Pallas kernels for 0%

commit v1 on v0

--- a/solution.py
+++ b/solution.py
@@ -14,7 +14,16 @@
     full_vector = lax.all_gather(right_vector, ("row", "col"), axis=0, tiled=True)
     permuted = jnp.take(column_panel, pivots, axis=0)
     moved = jnp.take(full_vector, pivots, axis=0)
-    segment = lax.all_gather(left_block, "col", axis=1, tiled=True)
+    ways = lax.axis_size("col")
+    up = [(d, (d + 1) % ways) for d in range(ways)]
+    down = [(d, (d - 1) % ways) for d in range(ways)]
+    earlier_2, later = ([left_block], [left_block])
+    for _ in range(ways // 2):
+        earlier_2.append(lax.ppermute(earlier_2[-1], "col", up))
+    for _ in range((ways - 1) // 2):
+        later.append(lax.ppermute(later[-1], "col", down))
+    line = jnp.concatenate([*earlier_2[::-1], *later[1:]], axis=1)
+    segment = jnp.roll(line, (lax.axis_index("col") - ways // 2) * left_block.shape[1], axis=1)
     product = jnp.dot(segment, permuted, preferred_element_type=jnp.float32)
     applied = jnp.dot(segment, moved, preferred_element_type=jnp.float32)
     share_size = added.shape[0]

time: 395 us -> 509 us (1.29); the launches traced: 394 us -> 501 us
  other arithmetic: 1.19 us -> 52.4 us
  starting transfers between devices: 2.26 us -> 31.7 us
  waiting for transfers between devices: 54.3 us -> 76.7 us
  matrix products: 27.2 us -> 21.4 us
    concatenate x0 -> x5, other arithmetic: none -> 51.3 us  [compose(): jnp.roll(line, (lax.axis_index('col') - ways // 2) * left_block.shape[1],...]
    ppermute x0 -> x15, waiting for transfers between devices: none -> 40.9 us  [the longest x10 40.9 us: compose(): earlier_2.append(lax.ppermute(earlier_2[-1], 'col', up))]
    ppermute x0 -> x15, starting transfers between devices: none -> 30.6 us  [the longest x10 23.7 us: compose(): earlier_2.append(lax.ppermute(earlier_2[-1], 'col', up))]
    all_gather x5 -> x0, waiting for transfers between devices: 14.1 us -> none  [compose(): segment = lax.all_gather(left_block, 'col', axis=1, tiled=True)]
    gather x5, local copies, waits for them, and re-layouts: 46.4 us -> 51.8 us  [compose(): permuted = jnp.take(column_panel, pivots, axis=0)]
    all_gather x5, blocking collectives: 169 us -> 174 us  [compose(): lax.all_gather(right_vector, ('row', 'col'), axis=0, tiled=True)]
  transfers between devices with their start and end apart: 14 -> 24, of which waited for: 7 -> 9; matrix products, arithmetic and copies ran while one was open for 30% -> 24% of each run, Pallas kernels for 0% -> 0%
where the time goes in v1:
time: 509 us; the launch traced here: 501 us
  blocking collectives  174 us (34%)
  local copies, waits for them, and re-layouts  130 us (26%)
  waiting for transfers between devices  76.7 us (15%)
  other arithmetic  52.4 us (10%)
  starting transfers between devices  31.7 us (6%)
  matrix products  21.4 us (4%)
  between operations  14.4 us (3%)
    all_gather x5, blocking collectives, compose(): lax.all_gather(right_vector, ('row', 'col'), axis=0, tiled=True)  174 us
    gather x5, local copies, waits for them, and re-layouts, compose(): moved = jnp.take(full_vector, pivots, axis=0)  65.4 us
    gather x5, local copies, waits for them, and re-layouts, compose(): permuted = jnp.take(column_panel, pivots, axis=0)  51.8 us
    concatenate x5, other arithmetic, compose(): jnp.roll(line, (lax.axis_index('col') - ways // 2) * left_block.shape[1],...  51.3 us
    ppermute x10, waiting for transfers between devices, compose(): earlier_2.append(lax.ppermute(earlier_2[-1], 'col', up))  40.9 us
    ppermute x4, waiting for transfers between devices, from_behind(): lax.ppermute(value, axis, [(i, (i + by) % devices) for i in range(devices)])  35.7 us
    ppermute x10, starting transfers between devices, compose(): earlier_2.append(lax.ppermute(earlier_2[-1], 'col', up))  23.7 us
    dot_general x5, matrix products, compose(): product = jnp.dot(segment, permuted, preferred_element_type=jnp.float32)  18.7 us
  transfers between devices with their start and end apart: 24, of which 9 were waited for; matrix products, arithmetic and copies ran while one was open for 24% of the time, Pallas kernels for 0%

profile of v1, /device:TPU:8, one launch (start us, length us, event | category | flops | bytes accessed | tf_op | source)
XLA Modules:
  0.0 500.8 jit_solution(13373064167385995998)
XLA Ops:
  12.1 11.4 %collective-permute-done.6 = bf16[512,512]{1,0:T(8,128)(2,1)S(1)} collective-permute-done((bf16[512,512]{1,0:T(8,128)(2,1)S(1)}, bf16[512,512]{1,0:T(8,128)(2,1)S(1)}, u32[]{:S(2)}, u32[]{:S(2)}) %collective-permute-start.6) | collective-permute-done | bytes 524320 | tf_op jit(solution)/shard_map/ppermute | solution.py:22
  25.1 35.1 %all-gather.1 = bf16[1,1,2048]{2,1,0:T(2,128)(2,1)S(1)} all-gather(bf16[1,1,128]{2,1,0:T(2,128)(2,1)S(1)} %slice.51), channel_id=3, replica_groups=mesh['loop'=16,'row'=4,'col'=4] {'row','col'}, dimensions={2}, use_global_device_ids=true | all-gather | bytes 4352 | tf_op jit(solution)/shard_map/all_gather | solution.py:14
  60.2 13.1 %gather_fusion.5 = bf16[2048]{0:T(1024)(128)(2,1)S(1)} fusion(bf16[2048]{0:T(1024)(128)(2,1)S(1)} %reduce, s32[2048]{0:T(1024)S(1)} %fusion.73), kind=kCustom, calls=%fused_computation.1.clone | custom fusion | bytes 16384 | tf_op jit(solution)/shard_map/jit(_take)/gather | solution.py:16
  74.2 4.1 fusion.17
  78.3 11.1 %gather_fusion = bf16[2048,512]{1,0:T(8,128)(2,1)} fusion(bf16[2048,512]{1,0:T(8,128)(2,1)} %bitcast.59, s32[2048]{0:T(1024)S(1)} %fusion.73), kind=kCustom, calls=%fused_computation.clone | custom fusion | bytes 4202496 | tf_op jit(solution)/shard_map/jit(_take)/gather | solution.py:15
  97.8 7.4 %collective-permute-done.3 = bf16[512,512]{1,0:T(8,128)(2,1)} collective-permute-done((bf16[512,512]{1,0:T(8,128)(2,1)S(1)}, bf16[512,512]{1,0:T(8,128)(2,1)}, u32[]{:S(2)}, u32[]{:S(2)}) %collective-permute-start.3) | collective-permute-done | bytes 524320 | tf_op jit(solution)/shard_map/ppermute | solution.py:22
  107.9 35.9 %all-gather.2 = bf16[16,1,128]{2,1,0:T(2,128)(2,1)S(1)} all-gather(bf16[1,1,128]{2,1,0:T(2,128)(2,1)S(1)} %fusion.82), channel_id=1, replica_groups=mesh['loop'=16,'row'=4,'col'=4] {'row','col'}, dimensions={0}, use_global_device_ids=true | all-gather | bytes 4352 | tf_op jit(solution)/shard_map/all_gather | solution.py:14
  143.9 13.1 %gather_fusion.6 = bf16[2048]{0:T(1024)(128)(2,1)S(1)} fusion(bf16[2048]{0:T(1024)(128)(2,1)S(1)} %bitcast.56, s32[2048]{0:T(1024)S(1)} %fusion.74), kind=kCustom, calls=%fused_computation.6.clone | custom fusion | bytes 16384 | tf_op jit(solution)/shard_map/jit(_take)/gather | solution.py:16
  157.0 3.9 fusion.24
  161.0 11.1 %gather_fusion.1 = bf16[2048,512]{1,0:T(8,128)(2,1)} fusion(bf16[2048,512]{1,0:T(8,128)(2,1)} %all-gather.12.cloned.1.call-done, s32[2048]{0:T(1024)S(1)} %fusion.74), kind=kCustom, calls=%fused_computation.2.clone | custom fusion | bytes 4202496 | tf_op jit(solution)/shard_map/jit(_take)/gather | solution.py:15
  181.0 7.1 %collective-permute-done = bf16[512,512]{1,0:T(8,128)(2,1)S(1)} collective-permute-done((bf16[512,512]{1,0:T(8,128)(2,1)S(1)}, bf16[512,512]{1,0:T(8,128)(2,1)S(1)}, u32[]{:S(2)}, u32[]{:S(2)}) %collective-permute-start) | collective-permute-done | bytes 524320 | tf_op jit(solution)/shard_map/ppermute | solution.py:22
  191.0 35.7 %all-gather.3 = bf16[16,1,128]{2,1,0:T(2,128)(2,1)S(1)} all-gather(bf16[1,1,128]{2,1,0:T(2,128)(2,1)S(1)} %fusion.80), channel_id=1, replica_groups=mesh['loop'=16,'row'=4,'col'=4] {'row','col'}, dimensions={0}, use_global_device_ids=true | all-gather | bytes 4352 | tf_op jit(solution)/shard_map/all_gather | solution.py:14
  226.7 13.1 %gather_fusion.7 = bf16[2048]{0:T(1024)(128)(2,1)S(1)} fusion(bf16[2048]{0:T(1024)(128)(2,1)S(1)} %bitcast.57, s32[2048]{0:T(1024)S(1)} %fusion.75), kind=kCustom, calls=%fused_computation.7.clone | custom fusion | bytes 16384 | tf_op jit(solution)/shard_map/jit(_take)/gather | solution.py:16
  239.9 3.8 fusion.31
  243.7 11.1 %gather_fusion.2 = bf16[2048,512]{1,0:T(8,128)(2,1)} fusion(bf16[2048,512]{1,0:T(8,128)(2,1)} %all-gather.14.cloned.1.call-done, s32[2048]{0:T(1024)S(1)} %fusion.75), kind=kCustom, calls=%fused_computation.3.clone | custom fusion | bytes 4202496 | tf_op jit(solution)/shard_map/jit(_take)/gather | solution.py:15
  258.6 15.0 %collective-permute-done.12 = bf16[512,512]{0,1:T(8,128)(2,1)S(1)} collective-permute-done((bf16[512,512]{0,1:T(8,128)(2,1)S(1)}, bf16[512,512]{0,1:T(8,128)(2,1)S(1)}, u32[]{:S(2)}, u32[]{:S(2)}) %collective-permute-start.12) | collective-permute-done | bytes 524320 | tf_op jit(solution)/shard_map/ppermute | solution.py:9
  278.6 6.8 %collective-permute-done.9 = bf16[512,512]{0,1:T(8,128)(2,1)S(1)} collective-permute-done((bf16[512,512]{0,1:T(8,128)(2,1)S(1)}, bf16[512,512]{0,1:T(8,128)(2,1)S(1)}, u32[]{:S(2)}, u32[]{:S(2)}) %collective-permute-start.9) | collective-permute-done | bytes 524320 | tf_op jit(solution)/shard_map/ppermute | solution.py:22
  288.2 5.6 %collective-permute-done.17 = bf16[128]{0:T(256)(128)(2,1)S(1)} collective-permute-done((bf16[128]{0:T(256)(128)(2,1)S(1)}, bf16[128]{0:T(256)(128)(2,1)S(1)}, u32[]{:S(2)}, u32[]{:S(2)}) %collective-permute-start.17) | collective-permute-done | bytes 288 | tf_op jit(solution)/shard_map/ppermute | solution.py:9
  293.8 33.9 %all-gather.4 = bf16[16,1,128]{2,1,0:T(2,128)(2,1)S(1)} all-gather(bf16[1,1,128]{2,1,0:T(2,128)(2,1)S(1)} %bitcast.76), channel_id=1, replica_groups=mesh['loop'=16,'row'=4,'col'=4] {'row','col'}, dimensions={0}, use_global_device_ids=true | all-gather | bytes 4352 | tf_op jit(solution)/shard_map/all_gather | solution.py:14
  327.7 13.1 %gather_fusion.8 = bf16[2048]{0:T(1024)(128)(2,1)S(1)} fusion(bf16[2048]{0:T(1024)(128)(2,1)S(1)} %bitcast.58, s32[2048]{0:T(1024)S(1)} %fusion.76), kind=kCustom, calls=%fused_computation.8.clone | custom fusion | bytes 16384 | tf_op jit(solution)/shard_map/jit(_take)/gather | solution.py:16
  340.9 20.3 %fusion.10 = bf16[512,2048]{0,1:T(8,128)(2,1)} fusion(s32[]{:T(128)S(6)} %select_n.72, bf16[512,512]{0,1:T(8,128)(2,1)S(1)} %collective-permute-done.10, bf16[512,512]{0,1:T(8,128)(2,1)S(1)} %collective-permute-done.9, bf16[512,512]{0,1:T(8,128)(2,1)S(1)} %fusion.56, bf16[512,512]{0,1:T(8,128)(2,1)S(1)} %collective-permute-done.11), kind=kLoop, calls=%fused_computation.60 | loop fusion | flops 16777216 | bytes 4194308 | tf_op jit(solution)/shard_map/jit(_roll_dynamic)/concatenate | solution.py:26
  364.0 9.3 %gather_fusion.3 = bf16[2048,512]{1,0:T(8,128)(2,1)} fusion(bf16[2048,512]{1,0:T(8,128)(2,1)S(1)} %copy.10, s32[2048]{0:T(1024)S(1)} %fusion.76), kind=kCustom, calls=%fused_computation.4.clone | custom fusion | bytes 4202496 | tf_op jit(solution)/shard_map/jit(_take)/gather | solution.py:15
  373.4 3.9 fusion.59
  377.4 10.4 %collective-permute-done.16 = bf16[512,512]{0,1:T(8,128)(2,1)S(1)} collective-permute-done((bf16[512,512]{0,1:T(8,128)(2,1)S(1)}, bf16[512,512]{0,1:T(8,128)(2,1)S(1)}, u32[]{:S(2)}, u32[]{:S(2)}) %collective-permute-start.16) | collective-permute-done | bytes 524320 | tf_op jit(solution)/shard_map/ppermute | solution.py:9
  392.5 8.2 %collective-permute-done.13 = bf16[512,512]{0,1:T(8,128)(2,1)S(1)} collective-permute-done((bf16[512,512]{0,1:T(8,128)(2,1)S(1)}, bf16[512,512]{0,1:T(8,128)(2,1)S(1)}, u32[]{:S(2)}, u32[]{:S(2)}) %collective-permute-start.13) | collective-permute-done | bytes 524320 | tf_op jit(solution)/shard_map/ppermute | solution.py:22
  400.8 3.9 collective-permute-start.14
  404.8 4.7 collective-permute-done.18
  409.5 33.5 %all-gather.5 = bf16[16,1,128]{2,1,0:T(2,128)(2,1)S(1)} all-gather(bf16[1,1,128]{2,1,0:T(2,128)(2,1)S(1)} %bitcast.75), channel_id=1, replica_groups=mesh['loop'=16,'row'=4,'col'=4] {'row','col'}, dimensions={0}, use_global_device_ids=true | all-gather | bytes 4352 | tf_op jit(solution)/shard_map/all_gather | solution.py:14
  443.0 13.1 %gather_fusion.9 = bf16[2048]{0:T(1024)(128)(2,1)S(1)} fusion(bf16[2048]{0:T(1024)(128)(2,1)S(1)} %bitcast.55, s32[2048]{0:T(1024)S(1)} %fusion.77), kind=kCustom, calls=%fused_computation.9.clone | custom fusion | bytes 16384 | tf_op jit(solution)/shard_map/jit(_take)/gather | solution.py:16
  456.2 19.1 %fusion.3 = bf16[512,2048]{0,1:T(8,128)(2,1)S(1)} fusion(s32[]{:T(128)S(6)} %select_n.72, bf16[512,512]{0,1:T(8,128)(2,1)S(1)} %collective-permute-done.14, bf16[512,512]{0,1:T(8,128)(2,1)S(1)} %collective-permute-done.13, bf16[512,512]{0,1:T(8,128)(2,1)S(1)} %fusion.59, bf16[512,512]{0,1:T(8,128)(2,1)S(1)} %collective-permute-done.15), kind=kLoop, calls=%fused_computation.53 | loop fusion | flops 16777216 | bytes 4194308 | tf_op jit(solution)/shard_map/jit(_roll_dynamic)/concatenate | solution.py:26
  480.5 9.2 %gather_fusion.4 = bf16[2048,512]{1,0:T(8,128)(2,1)} fusion(bf16[2048,512]{1,0:T(8,128)(2,1)S(1)} %copy.11, s32[2048]{0:T(1024)S(1)} %fusion.77), kind=kCustom, calls=%fused_computation.5.clone | custom fusion | bytes 4202496 | tf_op jit(solution)/shard_map/jit(_take)/gather | solution.py:15
  489.7 4.3 fusion.65
  (100 shorter events, 55.1 us)
Async XLA Ops:
  7.2 17.9 %copy-start.7 = (s32[1,3,2048]{2,0,1:T(1,128)S(1)}, s32[1,3,2048]{2,0,1:T(1,128)}, u32[]{:S(2)}) copy-start(s32[1,3,2048]{2,0,1:T(1,128)} %param.11) | copy-start | bytes 73732
  7.2 17.9 %copy-start.8 = (bf16[1,4,128]{2,1,0:T(4,128)(2,1)S(1)}, bf16[1,4,128]{2,1,0:T(4,128)(2,1)}, u32[]{:S(2)}) copy-start(bf16[1,4,128]{2,1,0:T(4,128)(2,1)} %param.13) | copy-start | bytes 3076
  7.2 71.1 %all-gather.20.cloned.1.call-start = ((), (), s32[]{:S(2)}) async-start(), calls=%async_computation.4 | async-start | bytes 2621440 | tf_op jit(solution)/shard_map/all_gather | solution.py:13
  9.7 63.6 %copy-start.2 = (bf16[512,512]{1,0:T(8,128)(2,1)}, bf16[512,512]{1,0:T(8,128)(2,1)S(1)}, u32[]{:S(2)}) copy-start(bf16[512,512]{1,0:T(8,128)(2,1)S(1)} %get-tuple-element.18) | copy-start | bytes 1572868
  9.7 151.3 %all-gather.12.cloned.1.call-start = ((), (), s32[]{:S(2)}) async-start(), calls=%async_computation | async-start | bytes 2621440 | tf_op jit(solution)/shard_map/all_gather | solution.py:13
  9.8 13.7 %collective-permute-start.6 = (bf16[512,512]{1,0:T(8,128)(2,1)S(1)}, bf16[512,512]{1,0:T(8,128)(2,1)S(1)}, u32[]{:S(2)}, u32[]{:S(2)}) collective-permute-start(bf16[512,512]{1,0:T(8,128)(2,1)S(1)} %get-tuple-element.18), channel_id=1, source_target_pairs={{0,1},{1,2},{2,3},{3,0},{4,5},{5,6},{6,7},{7,4},{8,9},{9,10},{10,1... | collective-permute-start | bytes 1572872 | tf_op jit(solution)/shard_map/ppermute | solution.py:22
  11.4 61.9 %collective-permute-start.8 = (bf16[512,512]{1,0:T(8,128)(2,1)S(1)}, bf16[512,512]{1,0:T(8,128)(2,1)S(1)}, u32[]{:S(2)}, u32[]{:S(2)}) collective-permute-start(bf16[512,512]{1,0:T(8,128)(2,1)S(1)} %get-tuple-element.18), channel_id=1, source_target_pairs={{0,3},{1,0},{2,1},{3,2},{4,7},{5,4},{6,5},{7,6},{8,11},{9,8},{10,9... | collective-permute-start | bytes 1572872 | tf_op jit(solution)/shard_map/ppermute | solution.py:24
  23.5 49.8 %copy-start.3 = (bf16[512,512]{1,0:T(8,128)(2,1)}, bf16[512,512]{1,0:T(8,128)(2,1)S(1)}, u32[]{:S(2)}) copy-start(bf16[512,512]{1,0:T(8,128)(2,1)S(1)} %collective-permute-done.6) | copy-start | bytes 1572868
  23.5 50.7 %collective-permute-start.7 = (bf16[512,512]{1,0:T(8,128)(2,1)S(1)}, bf16[512,512]{1,0:T(8,128)(2,1)}, u32[]{:S(2)}, u32[]{:S(2)}) collective-permute-start(bf16[512,512]{1,0:T(8,128)(2,1)S(1)} %collective-permute-done.6), channel_id=1, source_target_pairs={{0,1},{1,2},{2,3},{3,0},{4,5},{5,6},{6,7},{7,4},{8,9},{9,10},{10,1... | collective-permute-start | bytes 1572872 | tf_op jit(solution)/shard_map/ppermute | solution.py:22
  73.3 0.8 copy-start.4
  93.2 150.5 %all-gather.14.cloned.1.call-start = ((), (), s32[]{:S(2)}) async-start(), calls=%async_computation.1 | async-start | bytes 2621440 | tf_op jit(solution)/shard_map/all_gather | solution.py:13
  93.2 12.0 %collective-permute-start.3 = (bf16[512,512]{1,0:T(8,128)(2,1)S(1)}, bf16[512,512]{1,0:T(8,128)(2,1)}, u32[]{:S(2)}, u32[]{:S(2)}) collective-permute-start(bf16[512,512]{1,0:T(8,128)(2,1)S(1)} %get-tuple-element.16), channel_id=1, source_target_pairs={{0,1},{1,2},{2,3},{3,0},{4,5},{5,6},{6,7},{7,4},{8,9},{9,10},{10,1... | collective-permute-start | bytes 1572872 | tf_op jit(solution)/shard_map/ppermute | solution.py:22
  95.0 62.0 %collective-permute-start.5 = (bf16[512,512]{1,0:T(8,128)(2,1)S(1)}, bf16[512,512]{1,0:T(8,128)(2,1)}, u32[]{:S(2)}, u32[]{:S(2)}) collective-permute-start(bf16[512,512]{1,0:T(8,128)(2,1)S(1)} %get-tuple-element.16), channel_id=1, source_target_pairs={{0,3},{1,0},{2,1},{3,2},{4,7},{5,4},{6,5},{7,6},{8,11},{9,8},{10,9... | collective-permute-start | bytes 1572872 | tf_op jit(solution)/shard_map/ppermute | solution.py:24
  105.2 51.8 %collective-permute-start.4 = (bf16[512,512]{1,0:T(8,128)(2,1)}, bf16[512,512]{1,0:T(8,128)(2,1)}, u32[]{:S(2)}, u32[]{:S(2)}) collective-permute-start(bf16[512,512]{1,0:T(8,128)(2,1)} %collective-permute-done.3), channel_id=1, source_target_pairs={{0,1},{1,2},{2,3},{3,0},{4,5},{5,6},{6,7},{7,4},{8,9},{9,10},{10,1... | collective-permute-start | bytes 1572872 | tf_op jit(solution)/shard_map/ppermute | solution.py:22
  175.8 185.3 %all-gather.16.cloned.1.call-start = ((), (), s32[]{:S(2)}) async-start(), calls=%async_computation.2 | async-start | bytes 2621440 | tf_op jit(solution)/shard_map/all_gather | solution.py:13
  175.9 12.2 %collective-permute-start = (bf16[512,512]{1,0:T(8,128)(2,1)S(1)}, bf16[512,512]{1,0:T(8,128)(2,1)S(1)}, u32[]{:S(2)}, u32[]{:S(2)}) collective-permute-start(bf16[512,512]{1,0:T(8,128)(2,1)S(1)} %get-tuple-element.17), channel_id=1, source_target_pairs={{0,1},{1,2},{2,3},{3,0},{4,5},{5,6},{6,7},{7,4},{8,9},{9,10},{10,1... | collective-permute-start | bytes 1572872 | tf_op jit(solution)/shard_map/ppermute | solution.py:22
  178.2 61.7 %collective-permute-start.2 = (bf16[512,512]{1,0:T(8,128)(2,1)S(1)}, bf16[512,512]{1,0:T(8,128)(2,1)}, u32[]{:S(2)}, u32[]{:S(2)}) collective-permute-start(bf16[512,512]{1,0:T(8,128)(2,1)S(1)} %get-tuple-element.17), channel_id=1, source_target_pairs={{0,3},{1,0},{2,1},{3,2},{4,7},{5,4},{6,5},{7,6},{8,11},{9,8},{10,9... | collective-permute-start | bytes 1572872 | tf_op jit(solution)/shard_map/ppermute | solution.py:24
  188.1 51.8 %collective-permute-start.1 = (bf16[512,512]{1,0:T(8,128)(2,1)S(1)}, bf16[512,512]{1,0:T(8,128)(2,1)}, u32[]{:S(2)}, u32[]{:S(2)}) collective-permute-start(bf16[512,512]{1,0:T(8,128)(2,1)S(1)} %collective-permute-done), channel_id=1, source_target_pairs={{0,1},{1,2},{2,3},{3,0},{4,5},{5,6},{6,7},{7,4},{8,9},{9,10},{10,1... | collective-permute-start | bytes 1572872 | tf_op jit(solution)/shard_map/ppermute | solution.py:22
  257.9 15.7 %collective-permute-start.12 = (bf16[512,512]{0,1:T(8,128)(2,1)S(1)}, bf16[512,512]{0,1:T(8,128)(2,1)S(1)}, u32[]{:S(2)}, u32[]{:S(2)}) collective-permute-start(bf16[512,512]{0,1:T(8,128)(2,1)S(1)} %fusion.56), channel_id=1, source_target_pairs={{0,16},{16,32},{32,48},{48,64},{64,80},{80,96},{96,112},{112,128},... | collective-permute-start | bytes 1572872 | tf_op jit(solution)/shard_map/ppermute | solution.py:9
  273.6 0.8 copy-start.5
  274.4 203.2 %all-gather.18.cloned.1.call-start = ((), (), s32[]{:S(2)}) async-start(), calls=%async_computation.3 | async-start | bytes 2621440 | tf_op jit(solution)/shard_map/all_gather | solution.py:13
  274.5 10.9 %collective-permute-start.9 = (bf16[512,512]{0,1:T(8,128)(2,1)S(1)}, bf16[512,512]{0,1:T(8,128)(2,1)S(1)}, u32[]{:S(2)}, u32[]{:S(2)}) collective-permute-start(bf16[512,512]{0,1:T(8,128)(2,1)S(1)} %fusion.56), channel_id=1, source_target_pairs={{0,1},{1,2},{2,3},{3,0},{4,5},{5,6},{6,7},{7,4},{8,9},{9,10},{10,1... | collective-permute-start | bytes 1572872 | tf_op jit(solution)/shard_map/ppermute | solution.py:22
  278.1 62.8 %collective-permute-start.11 = (bf16[512,512]{0,1:T(8,128)(2,1)S(1)}, bf16[512,512]{0,1:T(8,128)(2,1)S(1)}, u32[]{:S(2)}, u32[]{:S(2)}) collective-permute-start(bf16[512,512]{0,1:T(8,128)(2,1)S(1)} %fusion.56), channel_id=1, source_target_pairs={{0,3},{1,0},{2,1},{3,2},{4,7},{5,4},{6,5},{7,6},{8,11},{9,8},{10,9... | collective-permute-start | bytes 1572872 | tf_op jit(solution)/shard_map/ppermute | solution.py:24
  285.4 55.5 %collective-permute-start.10 = (bf16[512,512]{0,1:T(8,128)(2,1)S(1)}, bf16[512,512]{0,1:T(8,128)(2,1)S(1)}, u32[]{:S(2)}, u32[]{:S(2)}) collective-permute-start(bf16[512,512]{0,1:T(8,128)(2,1)S(1)} %collective-permute-done.9), channel_id=1, source_target_pairs={{0,1},{1,2},{2,3},{3,0},{4,5},{5,6},{6,7},{7,4},{8,9},{9,10},{10,1... | collective-permute-start | bytes 1572872 | tf_op jit(solution)/shard_map/ppermute | solution.py:22
  288.1 5.7 %collective-permute-start.17 = (bf16[128]{0:T(256)(128)(2,1)S(1)}, bf16[128]{0:T(256)(128)(2,1)S(1)}, u32[]{:S(2)}, u32[]{:S(2)}) collective-permute-start(bf16[128]{0:T(256)(128)(2,1)S(1)} %fusion.78), channel_id=1, source_target_pairs={{0,16},{16,32},{32,48},{48,64},{64,80},{80,96},{96,112},{112,128},... | collective-permute-start | bytes 776 | tf_op jit(solution)/shard_map/ppermute | solution.py:9
  373.4 18.8 %copy-start = (bf16[512,2048]{0,1:T(8,128)(2,1)S(1)}, bf16[512,2048]{0,1:T(8,128)(2,1)}, u32[]{:S(2)}) copy-start(bf16[512,2048]{0,1:T(8,128)(2,1)} %fusion.10) | copy-start | bytes 6291460
  377.3 10.5 %collective-permute-start.16 = (bf16[512,512]{0,1:T(8,128)(2,1)S(1)}, bf16[512,512]{0,1:T(8,128)(2,1)S(1)}, u32[]{:S(2)}, u32[]{:S(2)}) collective-permute-start(bf16[512,512]{0,1:T(8,128)(2,1)S(1)} %fusion.59), channel_id=1, source_target_pairs={{0,32},{16,48},{32,64},{48,80},{64,96},{80,112},{96,128},{112,144}... | collective-permute-start | bytes 1572872 | tf_op jit(solution)/shard_map/ppermute | solution.py:9
  388.5 12.2 %collective-permute-start.13 = (bf16[512,512]{0,1:T(8,128)(2,1)S(1)}, bf16[512,512]{0,1:T(8,128)(2,1)S(1)}, u32[]{:S(2)}, u32[]{:S(2)}) collective-permute-start(bf16[512,512]{0,1:T(8,128)(2,1)S(1)} %fusion.59), channel_id=1, source_target_pairs={{0,1},{1,2},{2,3},{3,0},{4,5},{5,6},{6,7},{7,4},{8,9},{9,10},{10,1... | collective-permute-start | bytes 1572872 | tf_op jit(solution)/shard_map/ppermute | solution.py:22
  392.5 63.6 %collective-permute-start.15 = (bf16[512,512]{0,1:T(8,128)(2,1)S(1)}, bf16[512,512]{0,1:T(8,128)(2,1)S(1)}, u32[]{:S(2)}, u32[]{:S(2)}) collective-permute-start(bf16[512,512]{0,1:T(8,128)(2,1)S(1)} %fusion.59), channel_id=1, source_target_pairs={{0,3},{1,0},{2,1},{3,2},{4,7},{5,4},{6,5},{7,6},{8,11},{9,8},{10,9... | collective-permute-start | bytes 1572872 | tf_op jit(solution)/shard_map/ppermute | solution.py:24
  400.8 55.4 %collective-permute-start.14 = (bf16[512,512]{0,1:T(8,128)(2,1)S(1)}, bf16[512,512]{0,1:T(8,128)(2,1)S(1)}, u32[]{:S(2)}, u32[]{:S(2)}) collective-permute-start(bf16[512,512]{0,1:T(8,128)(2,1)S(1)} %collective-permute-done.13), channel_id=1, source_target_pairs={{0,1},{1,2},{2,3},{3,0},{4,5},{5,6},{6,7},{7,4},{8,9},{9,10},{10,1... | collective-permute-start | bytes 1572872 | tf_op jit(solution)/shard_map/ppermute | solution.py:22
  404.8 4.8 collective-permute-start.18
  475.3 1.3 copy-start.1
  (1 other events, 0.8 us)
Sparse Core Ops, SparseCore 0:
  10.4 32.0 all-gather.19
  93.3 32.1 all-gather.11
  175.9 32.9 all-gather.13
  274.6 29.4 all-gather.15
  388.7 31.8 all-gather.17
